TPU v7x, 32 devices: a whole 2x2x4 slice. The times are simulated.
32 devices in a mesh: sample: 8 (over y, x, core), token: 4 (over z).
Axes of the slice: x: 2, y: 2, z: 4, core: 2. Of those that a mesh axis runs over, the one named last changes fastest.
Arguments:
- activations: bfloat16 [16, 416, 768], P('sample', 'token'), may hold values from -6 to 6
- single: bfloat16 [416, 384], P('token'), may hold values from -6 to 6
- noise_index: int32 [16], P('sample'), may hold values from 0 to 199
- token_mask: int32 [416], replicated, may hold values 0 or 1
- pair_bias: bfloat16 [416, 16, 416], P('token', None, 'sample'), may hold values from -36 to 400
- fourier_freq: float32 [256], replicated, may hold values from -5 to 5
- fourier_phase: float32 [256], replicated, may hold values from 0 to 1
- noise_weight: bfloat16 [256, 384], replicated, may hold values from -0.375 to 0.375
- ada_weight: bfloat16 [384, 2304], replicated, may hold values from -0.3125 to 0.3125
- qkvg_weight: bfloat16 [768, 3072], P(None, 'sample'), may hold values from -0.21875 to 0.21875
- out_weight: bfloat16 [768, 768], P(None, 'sample'), may hold values from -0.21875 to 0.21875
Outputs:
- updated: bfloat16 [16, 416, 768], P('sample', 'token')
All inputs are finite; a program needn't handle non-finite values.
Results may differ from a plain program's by a relative error of at most 0.008.
Values may be sent and summed in bfloat16 or wider, within the bound.
No kernel may reach another device: no remote copies, remote signals or barrier semaphores. Data moves between devices by JAX's collectives and lax.ppermute only.
A program may use at most 128 MiB of HBM per device.

v0:
```python
import math
import jax
import jax.numpy as jnp
from jax import lax
from jax.sharding import PartitionSpec as P

HEADS = 16
STEPS = 200
sigma_data = 16.0
sigma_top = 160.0
sigma_low = 0.0004
exponent = 7.0
mask_penalty = 1000000000.0
norm_eps = 1e-05


def layer_norm(values):
    center = jnp.mean(values, axis=-1, keepdims=True)
    deviation = values - center
    spread = jnp.mean(deviation * deviation, axis=-1, keepdims=True)
    return deviation * lax.rsqrt(spread + norm_eps)


def noise_embedding(noise_index, fourier_freq, fourier_phase, noise_weight):
    fraction = noise_index.astype(jnp.float32) / (STEPS - 1)
    top_root = sigma_top ** (1.0 / exponent)
    low_root = sigma_low ** (1.0 / exponent)
    level_base = top_root + fraction * (low_root - top_root)
    sigma_level = sigma_data * level_base**exponent
    log_level = 0.25 * jnp.log(sigma_level / sigma_data)
    angles = 2.0 * math.pi * (log_level[:, None] * fourier_freq[None, :] + fourier_phase[None, :])
    features = layer_norm(jnp.cos(angles)).astype(jnp.bfloat16)
    return jnp.dot(features, noise_weight, preferred_element_type=jnp.float32)


def body(
    activations,
    single,
    noise_index,
    token_mask,
    pair_bias,
    fourier_freq,
    fourier_phase,
    noise_weight,
    ada_weight,
    qkvg_weight,
    out_weight,
):
    samples, query_count, model_width = activations.shape
    head_size = model_width // HEADS
    inverse = 1.0 / math.sqrt(head_size)
    penalty = (token_mask.astype(jnp.float32) - 1.0) * mask_penalty
    embedded = noise_embedding(noise_index, fourier_freq, fourier_phase, noise_weight)
    condition = layer_norm(single.astype(jnp.float32)[None, :, :] + embedded[:, None, :]).astype(
        jnp.bfloat16
    )
    modulate = jnp.dot(
        condition.reshape(samples * query_count, -1), ada_weight, preferred_element_type=jnp.float32
    )
    scale_part = modulate[:, :model_width]
    shift_part = modulate[:, model_width : 2 * model_width]
    out_gate = modulate[:, 2 * model_width :]
    flat_in = activations.reshape(samples * query_count, model_width).astype(jnp.float32)
    normed = (jax.nn.sigmoid(scale_part) * layer_norm(flat_in) + shift_part).astype(jnp.bfloat16)
    projected = jnp.dot(
        normed,
        lax.all_gather(qkvg_weight, "sample", axis=1, tiled=True),
        preferred_element_type=jnp.float32,
    ).astype(jnp.bfloat16)
    query_part = projected[:, :model_width]
    gate_part = projected[:, 3 * model_width :]
    travelling = projected[:, model_width : 3 * model_width].reshape(
        samples, query_count, 2 * model_width
    )
    query_heads = query_part.reshape(samples, query_count, HEADS, head_size)
    bias_rows = lax.all_gather(pair_bias, "sample", axis=2, tiled=True)
    top_old = jnp.full((samples, query_count, HEADS), -1e30, jnp.float32)
    segment = lax.all_gather(travelling, "token", axis=1, tiled=True)
    split_pairs = segment.reshape(samples, segment.shape[1], 2, HEADS, head_size)
    key_heads = split_pairs[:, :, 0]
    value_heads = split_pairs[:, :, 1]
    bias_block = bias_rows.astype(jnp.float32)
    scores = (
        jnp.einsum("sqhe,skhe->sqhk", query_heads, key_heads, preferred_element_type=jnp.float32)
        * inverse
    )
    scores = scores + bias_block[None] + penalty
    top_new = jnp.maximum(top_old, jnp.max(scores, axis=-1))
    weights = jnp.exp(scores - top_new[..., None])
    total_new = jnp.sum(weights, axis=-1)
    sum_new = jnp.einsum(
        "sqhk,skhe->sqhe",
        weights.astype(jnp.bfloat16),
        value_heads,
        preferred_element_type=jnp.float32,
    )
    result = (top_new, total_new, sum_new)
    top_last, total_last, sum_last = result
    attended = (sum_last / total_last[..., None]).reshape(samples * query_count, model_width)
    gated_rows = (attended * jax.nn.sigmoid(gate_part.astype(jnp.float32))).astype(jnp.bfloat16)
    output = (
        jax.nn.sigmoid(out_gate)
        * jnp.dot(
            gated_rows,
            lax.all_gather(out_weight, "sample", axis=1, tiled=True),
            preferred_element_type=jnp.float32,
        )
    ).astype(jnp.bfloat16)
    return output.reshape(samples, query_count, model_width)


def solution(mesh):
    placed = (
        P("sample", "token", None),
        P("token", None),
        P("sample"),
        P(),
        P("token", None, "sample"),
        P(),
        P(),
        P(),
        P(),
        P(None, "sample"),
        P(None, "sample"),
    )
    return jax.shard_map(
        body, mesh=mesh, in_specs=placed, out_specs=P("sample", "token", None), check_vma=False
    )
```

profile of v0, /device:TPU:0, one launch (start us, length us, event | category | flops | bytes accessed | tf_op | source)
XLA Modules:
  0.0 169.0 jit_solution(5035369524353801720)
XLA Ops:
  6.5 0.0 copy-start
  6.5 0.0 copy-start.5
  6.5 0.0 all-gather.5.cloned.1.call-start
  6.5 0.7 all-gather.5.cloned.1.call-update
  7.3 0.0 all-gather.9.cloned.1.call-start
  7.3 0.7 all-gather.9.cloned.1.call-update
  8.0 0.0 all-gather.7.cloned.1.call-start
  8.1 0.7 log_multiply_fusion
  8.7 0.9 fusion.32
  9.7 0.9 multiply_reduce_fusion.2
  10.6 0.9 convert_element_type.47
  11.5 1.2 fusion.28
  12.7 0.1 add_reduce_fusion
  12.8 0.1 div.44
  12.9 0.2 multiply_reduce_fusion.1
  13.1 0.1 rsqrt.32
  13.2 1.1 convert_reduce_fusion
  14.3 0.1 div.49
  14.4 1.2 multiply_reduce_fusion
  15.6 0.1 rsqrt.34
  15.7 0.1 fusion.26
  15.8 0.0 copy-done
  15.8 0.7 fusion.33
  16.5 0.0 copy-start.3
  16.5 1.3 copy-done.3
  17.8 0.0 copy-done.5
  17.8 0.3 fusion.15
  18.1 0.0 copy-start.6
  18.1 33.6 %all-gather.5.cloned.1.call-done = bf16[768,3072]{1,0:T(8,128)(2,1)} async-done(((bf16[768,384]{1,0:T(8,128)(2,1)}), bf16[768,3072]{1,0:T(8,128)(2,1)}) %all-gather.5.cloned.1.call-update) | async-done | bytes 4718608 | tf_op jit(solution)/shard_map/all_gather | solution.py:67
  51.7 3.5 %convolution_convert_fusion = bf16[208,3072]{1,0:T(8,128)(2,1)S(1)} fusion(bf16[208,768]{1,0:T(8,128)(2,1)S(1)} %fusion.15, bf16[768,3072]{1,0:T(8,128)(2,1)} %all-gather.5.cloned.1.call-done), kind=kOutput, calls=%fused_computation.6 | convolution fusion | flops 982106112 | bytes 6316032 | tf_op jit(solution)/shard_map/dot_general | solution.py:65
  55.2 0.0 copy-start.4
  55.2 1.3 copy.35
  56.6 0.0 all-gather.7.cloned.1.call-update
  56.6 0.2 all-gather.11.cloned.1.call-start
  56.8 0.3 all-gather.11.cloned.1.call-update
  57.2 0.0 copy-done.6
  57.2 22.5 %all-gather.9.cloned.1.call-done = bf16[104,16,416]{0,1,2:T(8,128)(2,1)} async-done(((bf16[104,16,52]{0,1,2:T(8,128)(2,1)}), bf16[104,16,416]{0,1,2:T(8,128)(2,1)}) %all-gather.9.cloned.1.call-update) | async-done | bytes 1384464 | tf_op jit(solution)/shard_map/all_gather | solution.py:76
  79.7 3.6 %copy.41 = f32[104,16,416]{0,2,1:T(8,128)} copy(bf16[104,16,416]{0,1,2:T(8,128)(2,1)} %all-gather.9.cloned.1.call-done) | data formatting | bytes 4153344 | tf_op jit(solution)/shard_map/convert_element_type | solution.py:82
  83.3 0.0 copy-done.4
  83.3 1.0 reshape.108
  84.3 50.7 %all-gather.7.cloned.1.call-done = bf16[2,416,1536]{2,0,1:T(2,128)(2,1)} async-done(((bf16[2,104,1536]{2,0,1:T(2,128)(2,1)}), bf16[2,416,1536]{2,0,1:T(2,128)(2,1)}) %all-gather.7.cloned.1.call-update) | async-done | bytes 2555920 | tf_op jit(solution)/shard_map/all_gather | solution.py:78
  135.0 8.5 %copy.36 = bf16[2,416,1536]{1,2,0:T(8,128)(2,1)} copy(bf16[2,416,1536]{2,0,1:T(2,128)(2,1)} %all-gather.7.cloned.1.call-done) | data formatting | bytes 5111808 | tf_op jit(solution)/shard_map/all_gather | solution.py:78
  143.5 0.0 copy-start.1
  143.5 4.8 %fusion.3 = (f32[2,104,16]{1,2,0:T(8,128)S(1)}, f32[2,16,416,104]{3,2,1,0:T(8,128)S(1)}) fusion(f32[416]{0:T(512)S(1)} %add_multiply_fusion, f32[104,16,416]{0,2,1:T(8,128)} %copy.41, bf16[2,104,16,48]{3,2,1,0:T(8,128)(2,1)S(1)} %reshape.108, bf16[2,416,2,16,48]{1,4,3,2,0:T(8,128)(2,1)} %bitcast.58), kind=kOutput, calls=%fused_computation.5 | convolution fusion | flops 138441472 | bytes 10852992 | tf_op jit(solution)/shard_map/sqhe,skhe->sqhk/dot_general | solution.py:84
  148.3 0.0 copy-done.1
  148.3 0.0 copy-start.2
  148.3 2.2 %fusion.1 = f32[2,104,16]{1,2,0:T(8,128)S(1)} fusion(f32[2,16,416,104]{3,2,1,0:T(8,128)S(1)} %get-tuple-element.8, f32[2,104,16]{1,2,0:T(8,128)S(1)} %broadcast_maximum_fusion, f32[416]{0:T(512)S(1)} %add_multiply_fusion, f32[104,16,416]{0,2,1:T(8,128)S(1)} %copy-done.1), kind=kLoop, calls=%fused_computation.3 | loop fusion | flops 6918912 | bytes 8334976 | tf_op jit(solution)/shard_map/reduce_sum | solution.py:90
  150.5 0.0 copy-done.2
  150.5 3.1 %fusion.11 = f32[2,104,16,48]{1,3,2,0:T(8,128)} fusion(f32[2,16,416,104]{3,2,1,0:T(8,128)S(1)} %get-tuple-element.8, f32[2,104,16]{1,2,0:T(8,128)S(1)} %broadcast_maximum_fusion, f32[416]{0:T(512)S(1)} %add_multiply_fusion, f32[104,16,416]{0,2,1:T(8,128)S(1)} %copy-done.1, bf16[2,416,2,16,48]{1,4,3,2,0:T(8,128)(2,1)S(1)} %bitcast.59, ...), kind=kOutput, calls=%fused_computation.14 | convolution fusion | flops 139988992 | bytes 12470272 | tf_op jit(solution)/shard_map/sqhk,skhe->sqhe/dot_general | solution.py:91
  153.6 1.9 %copy.48 = f32[2,104,16,48]{3,2,1,0:T(8,128)S(1)} copy(f32[2,104,16,48]{1,3,2,0:T(8,128)} %fusion.11) | data formatting | bytes 1277952 | tf_op jit(solution)/shard_map/reshape | solution.py:99
  155.5 1.5 reshape.109
  157.1 2.4 %all-gather.11.cloned.1.call-done = bf16[768,768]{0,1:T(8,128)(2,1)} async-done(((bf16[768,96]{0,1:T(8,128)(2,1)}), bf16[768,768]{0,1:T(8,128)(2,1)}) %all-gather.11.cloned.1.call-update) | async-done | bytes 1179664 | tf_op jit(solution)/shard_map/all_gather | solution.py:105
  159.4 3.0 %fusion.10 = bf16[208,768]{1,0:T(8,128)(2,1)} fusion(bf16[768,768]{0,1:T(8,128)(2,1)} %all-gather.11.cloned.1.call-done, f32[208,2304]{1,0:T(8,128)} %copy-done.3, f32[208,768]{1,0:T(8,128)} %reshape.109, bf16[208,3072]{1,0:T(8,128)(2,1)} %copy-done.4), kind=kOutput, calls=%fused_computation.13 | convolution fusion | flops 247123968 | bytes 3096576 | tf_op jit(solution)/shard_map/dot_general | solution.py:103
  (10 shorter events, 0.1 us)
Async XLA Ops:
  6.5 9.3 %copy-start = (bf16[384,2304]{1,0:T(8,128)(2,1)S(1)}, bf16[384,2304]{1,0:T(8,128)(2,1)}, u32[]{:S(2)}) copy-start(bf16[384,2304]{1,0:T(8,128)(2,1)} %param.19) | copy-start | bytes 5308420
  6.5 11.3 %copy-start.5 = (bf16[2,104,768]{2,1,0:T(8,128)(2,1)S(1)}, bf16[2,104,768]{2,1,0:T(8,128)(2,1)}, u32[]{:S(2)}) copy-start(bf16[2,104,768]{2,1,0:T(8,128)(2,1)} %param.11) | copy-start | bytes 958468
  6.5 45.1 %all-gather.5.cloned.1.call-start = ((), (), s32[]{:S(2)}) async-start(), calls=%async_computation | async-start | bytes 5308416 | tf_op jit(solution)/shard_map/all_gather | solution.py:67
  7.3 72.4 %all-gather.9.cloned.1.call-start = ((), (), s32[]{:S(2)}) async-start(), calls=%async_computation.2 | async-start | bytes 1916928 | tf_op jit(solution)/shard_map/all_gather | solution.py:76
  8.0 127.0 %all-gather.7.cloned.1.call-start = ((), (), s32[]{:S(2)}) async-start(), calls=%async_computation.1 | async-start | bytes 3194880 | tf_op jit(solution)/shard_map/all_gather | solution.py:78
  16.5 1.3 copy-start.3
  18.1 39.1 %copy-start.6 = (s32[416]{0:T(512)S(1)}, s32[416]{0:T(512)}, u32[]{:S(2)}) copy-start(s32[416]{0:T(512)} %param.14) | copy-start | bytes 4996
  55.2 28.1 %copy-start.4 = (bf16[208,3072]{1,0:T(8,128)(2,1)}, bf16[208,3072]{1,0:T(8,128)(2,1)S(1)}, u32[]{:S(2)}) copy-start(bf16[208,3072]{1,0:T(8,128)(2,1)S(1)} %convolution_convert_fusion) | copy-start | bytes 3833860
  56.6 102.9 %all-gather.11.cloned.1.call-start = ((), (), s32[]{:S(2)}) async-start(), calls=%async_computation.3 | async-start | bytes 1327104 | tf_op jit(solution)/shard_map/all_gather | solution.py:105
  143.5 4.8 %copy-start.1 = (f32[104,16,416]{0,2,1:T(8,128)S(1)}, f32[104,16,416]{0,2,1:T(8,128)}, u32[]{:S(2)}) copy-start(f32[104,16,416]{0,2,1:T(8,128)} %copy.41) | copy-start | bytes 8306692
  148.3 2.2 %copy-start.2 = (bf16[2,416,1536]{1,2,0:T(8,128)(2,1)S(1)}, bf16[2,416,1536]{1,2,0:T(8,128)(2,1)}, u32[]{:S(2)}) copy-start(bf16[2,416,1536]{1,2,0:T(8,128)(2,1)} %copy.36) | copy-start | bytes 7667716
Sparse Core Ops, SparseCore 0:
  9.2 42.4 all-gather.4
  53.5 26.1 all-gather.8
  81.3 53.6 all-gather.6
  136.7 22.6 all-gather.10
where the time goes:
time: 170 us; the launch traced here: 169 us
  waiting for transfers between devices  111 us (65%)
  local copies, waits for them, and re-layouts  19.6 us (12%)
  matrix products  16.3 us (10%)
  between operations  13.3 us (8%)
  other arithmetic  8.68 us (5%)
    all_gather x1, waiting for transfers between devices, body(): segment = lax.all_gather(travelling, 'token', axis=1, tiled=True)  50.7 us
    all_gather x1, waiting for transfers between devices, body(): lax.all_gather(qkvg_weight, 'sample', axis=1, tiled=True)  33.6 us
    all_gather x1, waiting for transfers between devices, body(): bias_rows = lax.all_gather(pair_bias, 'sample', axis=2, tiled=True)  22.5 us
    all_gather x1, local copies, waits for them, and re-layouts, body(): segment = lax.all_gather(travelling, 'token', axis=1, tiled=True)  8.52 us
    dot_general x1, matrix products, body(): jnp.einsum('sqhe,skhe->sqhk', query_heads, key_heads, preferred_element_t...  4.79 us
    convert_element_type x1, local copies, waits for them, and re-layouts, body(): bias_block = bias_rows.astype(jnp.float32)  3.56 us
    dot_general x1, matrix products, body(): jnp.dot(normed, lax.all_gather(qkvg_weight, 'sample', axis=1, tiled=True)...  3.51 us
    reshape x2, local copies, waits for them, and re-layouts, body(): (sum_last / total_last[..., None]).reshape(samples * query_count, model_w...  3.45 us
  transfers between devices with their start and end apart: 4, of which 4 were waited for; matrix products, arithmetic and copies ran while one was open for 24% of the time, Pallas kernels for 0%

commit v1 on v0

--- a/solution.py
+++ b/solution.py
@@ -75,7 +75,13 @@
     query_heads = query_part.reshape(samples, query_count, HEADS, head_size)
     bias_rows = lax.all_gather(pair_bias, "sample", axis=2, tiled=True)
     top_old = jnp.full((samples, query_count, HEADS), -1e30, jnp.float32)
-    segment = lax.all_gather(travelling, "token", axis=1, tiled=True)
+    size = lax.axis_size("token")
+    held, blocks = (travelling, [travelling])
+    for _ in range(size - 1):
+        held = lax.ppermute(held, "token", [(i, (i + 1) % size) for i in range(size)])
+        blocks.insert(0, held)
+    row_of_blocks = jnp.concatenate(blocks, axis=1)
+    segment = jnp.roll(row_of_blocks, (lax.axis_index("token") + 1) * travelling.shape[1], axis=1)
     split_pairs = segment.reshape(samples, segment.shape[1], 2, HEADS, head_size)
     key_heads = split_pairs[:, :, 0]
     value_heads = split_pairs[:, :, 1]

time: 170 us -> 148 us (0.87)
  waiting for transfers between devices: 111 us -> 75.2 us
  local copies, waits for them, and re-layouts: 19.6 us -> 31.8 us
    all_gather x1 -> x0, waiting for transfers between devices: 50.7 us -> none  [body(): segment = lax.all_gather(travelling, 'token', axis=1, tiled=True)]
    ppermute x0 -> x3, waiting for transfers between devices: none -> 41.5 us  [body(): lax.ppermute(held, 'token', [(i, (i + 1) % size) for i in range(size)])]
    all_gather x1, waiting for transfers between devices: 22.5 us -> 0.02 us  [body(): bias_rows = lax.all_gather(pair_bias, 'sample', axis=2, tiled=True)]
    concatenate x0 -> x1, local copies, waits for them, and re-layouts: none -> 9.86 us  [body(): jnp.roll(row_of_blocks, (lax.axis_index('token') + 1) * travelling.shape[...]
    all_gather x1 -> x0, local copies, waits for them, and re-layouts: 8.52 us -> none  [body(): segment = lax.all_gather(travelling, 'token', axis=1, tiled=True)]
    ppermute x0 -> x3, local copies, waits for them, and re-layouts: none -> 6.07 us  [body(): lax.ppermute(held, 'token', [(i, (i + 1) % size) for i in range(size)])]
    dynamic_slice x0 -> x1, local copies, waits for them, and re-layouts: none -> 4.01 us  [body(): jnp.roll(row_of_blocks, (lax.axis_index('token') + 1) * travelling.shape[...]
    dot_general x1, matrix products: 4.79 us -> 2.29 us  [body(): jnp.einsum('sqhe,skhe->sqhk', query_heads, key_heads, preferred_element_t...]
  transfers between devices with their start and end apart: 4 -> 6, of which waited for: 4 -> 4; matrix products, arithmetic and copies ran while one was open for 24% -> 35% of each run, Pallas kernels for 0% -> 0%
where the time goes in v1:
time: 148 us; the launch traced here: 147 us
  waiting for transfers between devices  75.2 us (51%)
  local copies, waits for them, and re-layouts  31.8 us (21%)
  matrix products  15.2 us (10%)
  between operations  13.3 us (9%)
  other arithmetic  10 us (7%)
  starting transfers between devices  1.63 us (1%)
    ppermute x3, waiting for transfers between devices, body(): lax.ppermute(held, 'token', [(i, (i + 1) % size) for i in range(size)])  41.5 us
    all_gather x1, waiting for transfers between devices, body(): lax.all_gather(qkvg_weight, 'sample', axis=1, tiled=True)  32.2 us
    concatenate x1, local copies, waits for them, and re-layouts, body(): jnp.roll(row_of_blocks, (lax.axis_index('token') + 1) * travelling.shape[...  9.86 us
    ppermute x3, local copies, waits for them, and re-layouts, body(): lax.ppermute(held, 'token', [(i, (i + 1) % size) for i in range(size)])  6.07 us
    dynamic_slice x1, local copies, waits for them, and re-layouts, body(): jnp.roll(row_of_blocks, (lax.axis_index('token') + 1) * travelling.shape[...  4.01 us
    convert_element_type x1, local copies, waits for them, and re-layouts, body(): bias_block = bias_rows.astype(jnp.float32)  3.66 us
    dot_general x1, matrix products, body(): jnp.dot(normed, lax.all_gather(qkvg_weight, 'sample', axis=1, tiled=True)...  3.56 us
    reshape x2, local copies, waits for them, and re-layouts, body(): (sum_last / total_last[..., None]).reshape(samples * query_count, model_w...  3.47 us
  transfers between devices with their start and end apart: 6, of which 4 were waited for; matrix products, arithmetic and copies ran while one was open for 35% of the time, Pallas kernels for 0%

profile of v1, /device:TPU:0, one launch (start us, length us, event | category | flops | bytes accessed | tf_op | source)
XLA Modules:
  0.0 147.1 jit_solution(17086643163549742535)
XLA Ops:
  6.5 0.0 copy-start
  6.5 0.0 copy-start.4
  6.5 0.0 all-gather.4.cloned.1.call-start
  6.5 0.7 all-gather.4.cloned.1.call-update
  7.3 0.0 all-gather.6.cloned.1.call-start
  7.3 0.7 all-gather.6.cloned.1.call-update
  8.0 0.0 all-gather.8.cloned.1.call-start
  8.1 0.7 log_multiply_fusion
  8.7 0.9 fusion.32
  9.7 0.9 multiply_reduce_fusion.2
  10.6 0.9 convert_element_type.47
  11.5 1.2 fusion.28
  12.7 0.1 add_reduce_fusion
  12.8 0.2 multiply_reduce_fusion.1
  13.0 0.1 div.44
  13.1 0.1 rsqrt.32
  13.2 1.1 convert_reduce_fusion
  14.3 1.2 multiply_reduce_fusion
  15.5 0.1 fusion.26
  15.6 0.0 copy-done
  15.7 2.0 %fusion.33 = f32[208,2304]{1,0:T(8,128)} fusion(bf16[208,384]{1,0:T(8,128)(2,1)S(1)} %fusion.26, bf16[384,2304]{1,0:T(8,128)(2,1)S(1)} %copy-done), kind=kOutput, calls=%fused_computation.58 | convolution fusion | flops 368050176 | bytes 3846144 | tf_op jit(solution)/shard_map/dot_general | solution.py:57
  17.6 0.1 div.49
  17.7 0.1 rsqrt.34
  17.8 0.0 copy-done.4
  17.8 1.7 %fusion.15 = bf16[208,768]{1,0:T(8,128)(2,1)S(1)} fusion(f32[208,2304]{1,0:T(8,128)} %fusion.33, bf16[2,104,768]{2,1,0:T(8,128)(2,1)S(1)} %copy-done.4, f32[208]{0:T(256)S(1)} %rsqrt.34, f32[208]{0:T(256)S(1)} %div.49), kind=kLoop, calls=%fused_computation.17 | loop fusion | flops 1437696 | bytes 1918592 | tf_op jit(solution)/shard_map/convert_element_type | solution.py:64
  19.5 0.0 copy-start.6
  19.5 32.2 %all-gather.4.cloned.1.call-done = bf16[768,3072]{1,0:T(8,128)(2,1)} async-done(((bf16[768,384]{1,0:T(8,128)(2,1)}), bf16[768,3072]{1,0:T(8,128)(2,1)}) %all-gather.4.cloned.1.call-update) | async-done | bytes 4718608 | tf_op jit(solution)/shard_map/all_gather | solution.py:67
  51.7 3.6 %convolution_convert_fusion = bf16[208,3072]{1,0:T(8,128)(2,1)S(1)} fusion(bf16[208,768]{1,0:T(8,128)(2,1)S(1)} %fusion.15, bf16[768,3072]{1,0:T(8,128)(2,1)} %all-gather.4.cloned.1.call-done), kind=kOutput, calls=%fused_computation.6 | convolution fusion | flops 982106112 | bytes 6316032 | tf_op jit(solution)/shard_map/dot_general | solution.py:65
  55.2 0.0 copy-start.2
  55.2 1.1 copy-done.2
  56.4 1.5 %collective-permute-start = (bf16[2,104,1536]{2,1,0:T(8,128)(2,1)S(1)}, bf16[2,104,1536]{2,1,0:T(8,128)(2,1)S(1)}, u32[]{:S(2)}, u32[]{:S(2)}) collective-permute-start(bf16[2,104,1536]{2,1,0:T(8,128)(2,1)S(1)} %bitcast.60), channel_id=1, source_target_pairs={{0,1},{1,2},{2,3},{3,0},{4,5},{5,6},{6,7},{7,4},{8,9},{9,10},{10,1... | collective-permute-start | bytes 1916936 | tf_op jit(solution)/shard_map/ppermute | solution.py:81
  58.0 16.8 %collective-permute-done = bf16[2,104,1536]{2,1,0:T(8,128)(2,1)S(1)} collective-permute-done((bf16[2,104,1536]{2,1,0:T(8,128)(2,1)S(1)}, bf16[2,104,1536]{2,1,0:T(8,128)(2,1)S(1)}, u32[]{:S(2)}, u32[]{:S(2)}) %collective-permute-start) | collective-permute-done | bytes 639008 | tf_op jit(solution)/shard_map/ppermute | solution.py:81
  74.8 0.0 copy-start.5
  74.8 0.9 copy-done.5
  75.7 0.0 collective-permute-start.1
  75.7 17.6 %collective-permute-done.1 = bf16[2,104,1536]{2,1,0:T(8,128)(2,1)} collective-permute-done((bf16[2,104,1536]{2,1,0:T(8,128)(2,1)S(1)}, bf16[2,104,1536]{2,1,0:T(8,128)(2,1)}, u32[]{:S(2)}, u32[]{:S(2)}) %collective-permute-start.1) | collective-permute-done | bytes 639008 | tf_op jit(solution)/shard_map/ppermute | solution.py:81
  93.3 0.0 collective-permute-start.2
  93.3 0.0 all-gather.8.cloned.1.call-update
  93.3 0.0 copy-done.6
  93.3 0.0 slice-start
  93.3 0.0 all-gather.6.cloned.1.call-done
  93.4 3.7 %copy.55 = f32[104,16,416]{0,2,1:T(8,128)} copy(bf16[104,16,416]{0,1,2:T(8,128)(2,1)} %all-gather.6.cloned.1.call-done) | data formatting | bytes 4153344 | tf_op jit(solution)/shard_map/convert_element_type | solution.py:88
  97.0 0.4 copy.46
  97.4 0.0 slice-done
  97.4 1.9 %reshape.108 = bf16[2,104,16,48]{3,2,1,0:T(8,128)(2,1)} reshape(bf16[208,768]{1,0:T(8,128)(2,1)S(1)} %slice-done) | data formatting | bytes 638976 | tf_op jit(solution)/shard_map/reshape | solution.py:75
  99.4 1.5 copy.45
  100.8 2.3 %copy.44 = bf16[2,104,1536]{1,2,0:T(8,128)(2,1)} copy(bf16[2,104,1536]{2,1,0:T(8,128)(2,1)} %collective-permute-done.1) | data formatting | bytes 1277952 | tf_op jit(solution)/shard_map/ppermute | solution.py:81
  103.1 7.1 %collective-permute-done.2 = bf16[2,104,1536]{2,1,0:T(8,128)(2,1)} collective-permute-done((bf16[2,104,1536]{2,1,0:T(8,128)(2,1)}, bf16[2,104,1536]{2,1,0:T(8,128)(2,1)}, u32[]{:S(2)}, u32[]{:S(2)}) %collective-permute-start.2) | collective-permute-done | bytes 639008 | tf_op jit(solution)/shard_map/ppermute | solution.py:81
  110.2 2.3 %copy.43 = bf16[2,104,1536]{1,2,0:T(8,128)(2,1)} copy(bf16[2,104,1536]{2,1,0:T(8,128)(2,1)} %collective-permute-done.2) | data formatting | bytes 1277952 | tf_op jit(solution)/shard_map/ppermute | solution.py:81
  112.5 9.9 %concatenate.6 = bf16[2,832,1536]{1,2,0:T(8,128)(2,1)} concatenate(bf16[2,104,1536]{1,2,0:T(8,128)(2,1)} %copy.43, bf16[2,104,1536]{1,2,0:T(8,128)(2,1)} %copy.44, bf16[2,104,1536]{1,2,0:T(8,128)(2,1)S(1)} %copy.45, bf16[2,104,1536]{1,2,0:T(8,128)(2,1)S(1)} %copy.46, bf16[2,104,1536]{1,2,0:T(8,128)(2,1)} %copy.43, bf16[2,104,1536]{1,2,0:T(8,128)(2,1)} %copy.44, ...), dimensions={1} | concatenate | bytes 10223616 | tf_op jit(solution)/shard_map/jit(_roll_dynamic)/concatenate | solution.py:84
  122.4 0.0 copy-start.1
  122.4 0.0 copy-start.3
  122.4 4.0 %constant_dynamic-slice_fusion = bf16[2,416,1536]{1,2,0:T(8,128)(2,1)S(1)} fusion(bf16[2,832,1536]{1,2,0:T(8,128)(2,1)} %concatenate.6, s32[]{:T(128)S(6)} %select_n.14), kind=kLoop, calls=%fused_computation.53 | loop fusion | bytes 5111812 | tf_op jit(solution)/shard_map/jit(_roll_dynamic)/dynamic_slice | solution.py:84
  126.4 0.0 copy-done.1
  126.4 0.0 copy-done.3
  126.4 2.3 %fusion.3 = (f32[2,104,16]{1,2,0:T(8,128)S(1)}, f32[2,16,416,104]{3,2,1,0:T(8,128)S(1)}) fusion(f32[416]{0:T(512)S(1)} %add_multiply_fusion, f32[104,16,416]{0,2,1:T(8,128)S(1)} %copy-done.1, bf16[2,104,16,48]{3,2,1,0:T(8,128)(2,1)S(1)} %copy-done.3, bf16[2,416,2,16,48]{1,4,3,2,0:T(8,128)(2,1)S(1)} %bitcast.58), kind=kOutput, calls=%fused_computation.5 | convolution fusion | flops 138441472 | bytes 11385856 | tf_op jit(solution)/shard_map/sqhe,skhe->sqhk/dot_general | solution.py:90
  128.8 2.2 %fusion.1 = f32[2,104,16]{1,2,0:T(8,128)S(1)} fusion(f32[2,16,416,104]{3,2,1,0:T(8,128)S(1)} %get-tuple-element.8, f32[2,104,16]{1,2,0:T(8,128)S(1)} %broadcast_maximum_fusion, f32[416]{0:T(512)S(1)} %add_multiply_fusion, f32[104,16,416]{0,2,1:T(8,128)S(1)} %copy-done.1), kind=kLoop, calls=%fused_computation.3 | loop fusion | flops 6918912 | bytes 8334976 | tf_op jit(solution)/shard_map/reduce_sum | solution.py:96
  130.9 3.1 %fusion.11 = f32[2,104,16,48]{1,3,2,0:T(8,128)} fusion(f32[2,16,416,104]{3,2,1,0:T(8,128)S(1)} %get-tuple-element.8, f32[2,104,16]{1,2,0:T(8,128)S(1)} %broadcast_maximum_fusion, f32[416]{0:T(512)S(1)} %add_multiply_fusion, f32[104,16,416]{0,2,1:T(8,128)S(1)} %copy-done.1, bf16[2,416,2,16,48]{1,4,3,2,0:T(8,128)(2,1)S(1)} %bitcast.59, ...), kind=kOutput, calls=%fused_computation.14 | convolution fusion | flops 139988992 | bytes 12470272 | tf_op jit(solution)/shard_map/sqhk,skhe->sqhe/dot_general | solution.py:97
  134.1 1.9 %copy.62 = f32[2,104,16,48]{3,2,1,0:T(8,128)S(1)} copy(f32[2,104,16,48]{1,3,2,0:T(8,128)} %fusion.11) | data formatting | bytes 1277952 | tf_op jit(solution)/shard_map/reshape | solution.py:105
  136.0 1.6 %reshape.109 = f32[208,768]{1,0:T(8,128)} reshape(f32[2,104,16,48]{3,2,1,0:T(8,128)S(1)} %copy.62) | data formatting | bytes 1277952 | tf_op jit(solution)/shard_map/reshape | solution.py:105
  137.5 0.0 all-gather.8.cloned.1.call-done
  137.5 3.0 %fusion.10 = bf16[208,768]{1,0:T(8,128)(2,1)} fusion(bf16[768,768]{0,1:T(8,128)(2,1)} %all-gather.8.cloned.1.call-done, f32[208,2304]{1,0:T(8,128)} %fusion.33, f32[208,768]{1,0:T(8,128)} %reshape.109, bf16[208,3072]{1,0:T(8,128)(2,1)} %copy-done.2), kind=kOutput, calls=%fused_computation.13 | convolution fusion | flops 247123968 | bytes 3096576 | tf_op jit(solution)/shard_map/dot_general | solution.py:109
  (9 shorter events, 0.1 us)
Async XLA Ops:
  6.5 9.1 %copy-start = (bf16[384,2304]{1,0:T(8,128)(2,1)S(1)}, bf16[384,2304]{1,0:T(8,128)(2,1)}, u32[]{:S(2)}) copy-start(bf16[384,2304]{1,0:T(8,128)(2,1)} %param.19) | copy-start | bytes 5308420
  6.5 11.3 %copy-start.4 = (bf16[2,104,768]{2,1,0:T(8,128)(2,1)S(1)}, bf16[2,104,768]{2,1,0:T(8,128)(2,1)}, u32[]{:S(2)}) copy-start(bf16[2,104,768]{2,1,0:T(8,128)(2,1)} %param.11) | copy-start | bytes 958468
  6.5 45.1 %all-gather.4.cloned.1.call-start = ((), (), s32[]{:S(2)}) async-start(), calls=%async_computation | async-start | bytes 5308416 | tf_op jit(solution)/shard_map/all_gather | solution.py:67
  7.3 86.1 %all-gather.6.cloned.1.call-start = ((), (), s32[]{:S(2)}) async-start(), calls=%async_computation.1 | async-start | bytes 1916928 | tf_op jit(solution)/shard_map/all_gather | solution.py:76
  8.0 129.5 %all-gather.8.cloned.1.call-start = ((), (), s32[]{:S(2)}) async-start(), calls=%async_computation.2 | async-start | bytes 1327104 | tf_op jit(solution)/shard_map/all_gather | solution.py:111
  19.5 73.9 %copy-start.6 = (s32[416]{0:T(512)S(1)}, s32[416]{0:T(512)}, u32[]{:S(2)}) copy-start(s32[416]{0:T(512)} %param.14) | copy-start | bytes 4996
  55.2 1.1 copy-start.2
  56.4 18.4 %collective-permute-start = (bf16[2,104,1536]{2,1,0:T(8,128)(2,1)S(1)}, bf16[2,104,1536]{2,1,0:T(8,128)(2,1)S(1)}, u32[]{:S(2)}, u32[]{:S(2)}) collective-permute-start(bf16[2,104,1536]{2,1,0:T(8,128)(2,1)S(1)} %bitcast.60), channel_id=1, source_target_pairs={{0,1},{1,2},{2,3},{3,0},{4,5},{5,6},{6,7},{7,4},{8,9},{9,10},{10,1... | collective-permute-start | bytes 1916936 | tf_op jit(solution)/shard_map/ppermute | solution.py:81
  74.8 0.9 copy-start.5
  75.7 17.6 %collective-permute-start.1 = (bf16[2,104,1536]{2,1,0:T(8,128)(2,1)S(1)}, bf16[2,104,1536]{2,1,0:T(8,128)(2,1)}, u32[]{:S(2)}, u32[]{:S(2)}) collective-permute-start(bf16[2,104,1536]{2,1,0:T(8,128)(2,1)S(1)} %collective-permute-done), channel_id=1, source_target_pairs={{0,1},{1,2},{2,3},{3,0},{4,5},{5,6},{6,7},{7,4},{8,9},{9,10},{10,1... | collective-permute-start | bytes 1916936 | tf_op jit(solution)/shard_map/ppermute | solution.py:81
  93.3 16.9 %collective-permute-start.2 = (bf16[2,104,1536]{2,1,0:T(8,128)(2,1)}, bf16[2,104,1536]{2,1,0:T(8,128)(2,1)}, u32[]{:S(2)}, u32[]{:S(2)}) collective-permute-start(bf16[2,104,1536]{2,1,0:T(8,128)(2,1)} %collective-permute-done.1), channel_id=1, source_target_pairs={{0,1},{1,2},{2,3},{3,0},{4,5},{5,6},{6,7},{7,4},{8,9},{9,10},{10,1... | collective-permute-start | bytes 1916936 | tf_op jit(solution)/shard_map/ppermute | solution.py:81
  93.3 4.1 %slice-start = ((bf16[208,3072]{1,0:T(8,128)(2,1)}), bf16[208,768]{1,0:T(8,128)(2,1)S(1)}, s32[]{:S(2)}) async-start(bf16[208,3072]{1,0:T(8,128)(2,1)} %copy-done.2), calls=%async_computation.3 | async-start | bytes 638976 | tf_op jit(solution)/shard_map/slice | solution.py:70
  122.4 4.0 %copy-start.1 = (f32[104,16,416]{0,2,1:T(8,128)S(1)}, f32[104,16,416]{0,2,1:T(8,128)}, u32[]{:S(2)}) copy-start(f32[104,16,416]{0,2,1:T(8,128)} %copy.55) | copy-start | bytes 8306692
  122.4 4.0 %copy-start.3 = (bf16[2,104,16,48]{3,2,1,0:T(8,128)(2,1)S(1)}, bf16[2,104,16,48]{3,2,1,0:T(8,128)(2,1)}, u32[]{:S(2)}) copy-start(bf16[2,104,16,48]{3,2,1,0:T(8,128)(2,1)} %reshape.108) | copy-start | bytes 958468
Sparse Core Ops, SparseCore 0:
  9.2 42.4 all-gather.3
  53.5 26.1 all-gather.5
  93.4 24.3 all-gather.7
